TPU v7x, 32 devices: a whole 2x2x4 slice. The times are simulated.
32 devices in a mesh: rep: 8 (over z, y), tp: 4 (over x, core).
Axes of the slice: x: 2, y: 2, z: 4, core: 2. Of those that a mesh axis runs over, the one named last changes fastest.
Arguments:
- image_grads: bfloat16 [32, 48, 1280], P('rep', 'tp'), may hold values from -6 to 6
- dest_rank: int32 [32], P('rep'), may hold values from 0 to 7, as said below
- dest_slot: int32 [32], P('rep'), may hold values from 0 to 7, as said below
- saved_inputs: bfloat16 [64, 48, 1280], P('rep'), may hold values from -6 to 6
- up_weight: bfloat16 [1280, 5120], P(None, 'tp'), may hold values from -0.15625 to 0.15625
- down_weight: bfloat16 [5120, 1280], P('tp'), may hold values from -0.078125 to 0.078125
- norm_gain: float32 [1280], replicated, may hold values from 0.25 to 1.75
Outputs:
- input_grads: bfloat16 [64, 48, 1280], P('rep', 'tp')
- up_grads: float32 [1280, 5120], P('rep', 'tp')
- down_grads: float32 [5120, 1280], P('tp', 'rep')
- gain_grads: float32 [1280], replicated
Inputs may be any that keep to these rules, and one draw needn't show every extreme that they name: `dest_rank`: the images of one index of rep go to different owners; each owner receives at most 8 images, and some owner receives exactly 8 in every draw. `dest_slot`: the images that one owner receives have distinct slots 0, 1, ... up to their count less one; other slots hold no image.
All inputs are finite; a program needn't handle non-finite values.
Results may differ from a plain program's by a relative error of at most 0.015.
Values may be sent and summed in bfloat16 or wider, within the bound.
No kernel may reach another device: no remote copies, remote signals or barrier semaphores. Data moves between devices by JAX's collectives and lax.ppermute only.
A program may use at most 128 MiB of HBM per device.

v0:
```python
import jax
import jax.numpy as jnp
from jax import lax
from jax.sharding import PartitionSpec as P

epsilon = 1e-05
gelu_c = 0.7978845608028654
gelu_a = 0.044715


def gelu_value(preact):
    inner = jnp.tanh(gelu_c * (preact + gelu_a * preact**3))
    return 0.5 * preact * (1.0 + inner)


def gelu_slope(preact):
    inner = jnp.tanh(gelu_c * (preact + gelu_a * preact**3))
    return 0.5 * (1.0 + inner) + 0.5 * preact * (1.0 - inner * inner) * gelu_c * (
        1.0 + 3.0 * gelu_a * preact * preact
    )


def outbound(images, dest_rank, dest_slot, groups, capacity):
    rank_ids = jnp.arange(groups, dtype=jnp.int32)
    one_hot = dest_rank[None, :] == rank_ids[:, None]
    packed = jnp.einsum(
        "ek,kpd->epd", one_hot.astype(jnp.bfloat16), images, preferred_element_type=jnp.float32
    ).astype(jnp.bfloat16)
    present = jnp.any(one_hot, axis=1)
    slot_sent = jnp.sum(jnp.where(one_hot, dest_slot[None, :], 0), axis=1) + jnp.where(
        present, 0, capacity
    )
    return (packed, slot_sent)


def compact(inbound, slot_recv, capacity):
    slot_ids = jnp.arange(capacity, dtype=jnp.int32)
    picker = (slot_recv[None, :] == slot_ids[:, None]).astype(jnp.bfloat16)
    return jnp.einsum("ce,epd->cpd", picker, inbound, preferred_element_type=jnp.float32).astype(
        jnp.bfloat16
    )


def local(image_grads, dest_rank, dest_slot, saved_inputs, up_weight, down_weight, norm_gain):
    groups = lax.axis_size("rep")
    capacity = saved_inputs.shape[0]
    patches = saved_inputs.shape[1]
    width = saved_inputs.shape[2]
    slab = image_grads.shape[1]
    packed, slot_sent = outbound(image_grads, dest_rank, dest_slot, groups, capacity)
    inbound, slot_recv = (
        lax.all_to_all(packed, "rep", split_axis=0, concat_axis=0, tiled=True),
        lax.all_to_all(slot_sent, "rep", split_axis=0, concat_axis=0, tiled=True),
    )
    routed = lax.all_gather(compact(inbound, slot_recv, capacity), "tp", axis=1, tiled=True)
    rows = capacity * patches
    grads = routed.reshape(rows, width)
    values = saved_inputs.reshape(rows, width).astype(jnp.float32)
    mean_v = jnp.mean(values, axis=1, keepdims=True)
    var_v = jnp.mean((values - mean_v) ** 2, axis=1, keepdims=True)
    inv_std = 1.0 / jnp.sqrt(var_v + epsilon)
    centred = (values - mean_v) * inv_std
    normed = (centred * norm_gain[None, :]).astype(jnp.bfloat16)
    preact = jnp.dot(normed, up_weight, preferred_element_type=jnp.float32)
    hidden = gelu_value(preact).astype(jnp.bfloat16)
    grad_hidden = jnp.dot(grads, down_weight.T, preferred_element_type=jnp.float32)
    grad_pre = (grad_hidden * gelu_slope(preact)).astype(jnp.bfloat16)
    down_local = jnp.dot(hidden.T, grads, preferred_element_type=jnp.float32)
    up_local = jnp.dot(normed.T, grad_pre, preferred_element_type=jnp.float32)
    partial_normed = jnp.dot(grad_pre, up_weight.T, preferred_element_type=jnp.float32)
    up_grads, down_grads = (
        lax.psum_scatter(
            up_local.astype(jnp.bfloat16), "rep", scatter_dimension=0, tiled=True
        ).astype(jnp.float32),
        lax.psum_scatter(
            down_local.astype(jnp.bfloat16), "rep", scatter_dimension=1, tiled=True
        ).astype(jnp.float32),
    )
    start = lax.axis_index("tp") * slab
    grad_normed = lax.psum(partial_normed.astype(jnp.bfloat16), "tp").astype(jnp.float32)
    gain_grads = lax.psum(jnp.sum(grad_normed * centred, axis=0), "rep")
    scaled = grad_normed * norm_gain[None, :]
    first = jnp.mean(scaled, axis=1, keepdims=True)
    second = jnp.mean(scaled * centred, axis=1, keepdims=True)
    result = grads.astype(jnp.float32) + inv_std * (scaled - first - centred * second)
    result = result.reshape(capacity, patches, width)
    input_grads = lax.dynamic_slice_in_dim(result, start, slab, 1).astype(jnp.bfloat16)
    return (input_grads, up_grads, down_grads, gain_grads)


def solution(mesh):
    in_specs = (
        P("rep", "tp", None),
        P("rep"),
        P("rep"),
        P("rep", None, None),
        P(None, "tp"),
        P("tp", None),
        P(),
    )
    out_specs = (P("rep", "tp", None), P("rep", "tp"), P("tp", "rep"), P())
    return jax.shard_map(local, mesh=mesh, in_specs=in_specs, out_specs=out_specs, check_vma=False)
```

profile of v0, /device:TPU:0, one launch (start us, length us, event | category | flops | bytes accessed | tf_op | source)
XLA Modules:
  0.0 227.4 jit_solution(4812168266985921151)
XLA Ops:
  8.0 0.0 copy-start
  8.0 0.0 copy-start.6
  8.0 0.0 copy-start.4
  8.0 0.0 copy-start.5
  8.0 0.9 fusion.26
  8.9 0.9 select_reduce_fusion
  9.9 0.7 copy.19
  10.5 7.3 %all-to-all-start = ((s32[8,1,1]{2,1,0:T(1,128)}), s32[8,1,1]{2,1,0:T(1,128)S(1)}, u32[]{:S(2)}, u32[]{:S(2)}) async-start(s32[8,1,1]{2,1,0:T(1,128)} %copy.19), calls=%async_computation | async-start | bytes 8192 | tf_op jit(solution)/shard_map/all_to_all | solution.py:53
  17.8 1.4 convert_reduce_fusion
  19.3 0.1 div.18
  19.3 1.6 multiply_reduce_fusion
  20.9 0.1 sqrt.6
  21.0 0.0 copy-done.6
  21.0 0.0 copy-done.4
  21.1 0.3 convolution_convert_fusion.4
  21.4 0.0 copy-done.5
  21.4 2.5 %multiply_convert_fusion.1 = bf16[384,1280]{1,0:T(8,128)(2,1)} fusion(bf16[8,48,1280]{2,1,0:T(8,128)(2,1)} %param.10, f32[1280]{0:T(1024)S(1)} %copy-done.5, f32[384]{0:T(512)S(1)} %div.18, f32[384]{0:T(512)S(1)} %sqrt.6), kind=kLoop, calls=%fused_computation.29 | loop fusion | flops 2457600 | bytes 1974272 | tf_op jit(solution)/shard_map/convert_element_type | solution.py:63
  23.9 0.8 copy.20
  24.7 0.0 all-to-all-done
  24.7 6.0 %all-to-all-start.1 = ((bf16[8,12,1280]{2,1,0:T(8,128)(2,1)}), bf16[8,12,1280]{2,1,0:T(8,128)(2,1)}, u32[]{:S(2)}, u32[]{:S(2)}) async-start(bf16[8,12,1280]{2,1,0:T(8,128)(2,1)} %copy.20), calls=%async_computation.1 | async-start | bytes 655360 | tf_op jit(solution)/shard_map/all_to_all | solution.py:52
  30.7 0.0 all-reduce.2.cloned.1.call-start
  30.7 0.0 copy-done
  30.7 4.0 %fusion.33 = f32[384,1280]{1,0:T(8,128)} fusion(bf16[384,1280]{1,0:T(8,128)(2,1)} %multiply_convert_fusion.1, bf16[1280,1280]{1,0:T(8,128)(2,1)S(1)} %copy-done), kind=kOutput, calls=%fused_computation.56 | convolution fusion | flops 1258291200 | bytes 6225920 | tf_op jit(solution)/shard_map/dot_general | solution.py:64
  34.7 0.2 reduce.2
  34.9 5.6 %all-to-all-done.1 = bf16[8,12,1280]{2,1,0:T(8,128)(2,1)} async-done(((bf16[8,12,1280]{2,1,0:T(8,128)(2,1)}), bf16[8,12,1280]{2,1,0:T(8,128)(2,1)}, u32[]{:S(2)}, u32[]{:S(2)}) %all-to-all-start.1) | async-done | bytes 245792 | tf_op jit(solution)/shard_map/all_to_all | solution.py:52
  40.5 0.0 copy-start.7
  40.5 1.3 convolution_convert_fusion.3
  41.9 9.7 %all_gather.3 = bf16[8,48,1280]{2,0,1:T(8,128)(2,1)S(1)} all-gather(bf16[8,12,1280]{2,0,1:T(8,128)(2,1)S(1)} %convolution_convert_fusion.3), channel_id=1, replica_groups=mesh['rep'=8,'tp'=4] {'tp'}, dimensions={1}, use_global_device_ids=true | all-gather | bytes 1228800 | tf_op jit(solution)/shard_map/all_gather | solution.py:55
  51.5 0.2 copy.22
  51.7 0.0 copy-start.2
  51.7 0.0 copy-done.7
  51.7 3.8 %fusion = bf16[384,1280]{1,0:T(8,128)(2,1)S(1)} fusion(bf16[384,1280]{1,0:T(8,128)(2,1)S(1)} %bitcast.33, bf16[1280,1280]{1,0:T(8,128)(2,1)S(1)} %copy-done.7, f32[384,1280]{1,0:T(8,128)} %fusion.33), kind=kOutput, calls=%fused_computation.5 | convolution fusion | flops 1267630080 | bytes 7208960 | tf_op jit(solution)/shard_map/dot_general | solution.py:66
  55.5 0.0 copy-done.2
  55.6 0.0 copy-start.8
  55.6 0.9 copy-done.8
  56.5 2.4 %convolution_convert_fusion.2 = bf16[384,1280]{1,0:T(8,128)(2,1)} fusion(bf16[384,1280]{1,0:T(8,128)(2,1)S(1)} %fusion, bf16[1280,1280]{1,0:T(8,128)(2,1)S(1)} %copy-done), kind=kOutput, calls=%fused_computation.6 | convolution fusion | flops 1258782720 | bytes 5242880 | tf_op jit(solution)/shard_map/dot_general | solution.py:70
  58.9 0.0 all-reduce.2.cloned.1.call-update
  59.0 0.0 reduce-scatter.3.cloned.1.call-start
  59.0 5.1 %convolution_convert_fusion.1 = bf16[1280,1280]{1,0:T(8,128)(2,1)} fusion(bf16[384,1280]{1,0:T(8,128)(2,1)} %multiply_convert_fusion.1, bf16[384,1280]{1,0:T(8,128)(2,1)} %copy-done.8), kind=kOutput, calls=%fused_computation.1 | convolution fusion | flops 1259929600 | bytes 5242880 | tf_op jit(solution)/shard_map/dot_general | solution.py:69
  64.1 0.0 reduce-scatter.3.cloned.1.call-update
  64.1 0.2 reduce-scatter.5.cloned.1.call-start
  64.4 5.5 %convolution_convert_fusion = bf16[1280,1280]{0,1:T(8,128)(2,1)} fusion(bf16[384,1280]{1,0:T(8,128)(2,1)} %bitcast.34, f32[384,1280]{1,0:T(8,128)} %fusion.33), kind=kOutput, calls=%fused_computation | convolution fusion | flops 1264353280 | bytes 6225920 | tf_op jit(solution)/shard_map/dot_general | solution.py:68
  69.9 0.0 reduce-scatter.5.cloned.1.call-update
  69.9 23.6 %all-reduce.2.cloned.1.call-done = bf16[384,1280]{1,0:T(8,128)(2,1)} async-done(((bf16[384,1280]{1,0:T(8,128)(2,1)}), bf16[384,1280]{1,0:T(8,128)(2,1)}) %all-reduce.2.cloned.1.call-update) | async-done | bytes 983056 | tf_op jit(solution)/shard_map/psum | solution.py:80
  93.5 0.0 copy-start.1
  93.5 0.0 copy-start.3
  93.5 2.6 %fusion.8 = (f32[1280]{0:T(1024)S(1)}, f32[384]{0:T(512)S(1)}, f32[384]{0:T(512)S(1)}) fusion(bf16[384,1280]{1,0:T(8,128)(2,1)} %all-reduce.2.cloned.1.call-done, bf16[8,48,1280]{2,1,0:T(8,128)(2,1)} %param.10, f32[384]{0:T(512)S(1)} %div.18, f32[384]{0:T(512)S(1)} %sqrt.6, f32[1280]{0:T(1024)S(1)} %copy-done.5), kind=kLoop, calls=%fused_computation.18 | loop fusion | flops 4913152 | bytes 1982464 | tf_op jit(solution)/shard_map/reduce_sum | solution.py:81
  96.1 0.0 copy-done.1
  96.1 0.0 copy-done.3
  96.1 2.1 fusion.6
  98.2 0.1 constant_dynamic-slice_fusion
  98.3 0.8 copy.28
  99.0 22.1 %psum.15 = f32[1280]{0:T(1024)} all-reduce(f32[1280]{0:T(1024)S(1)} %get-tuple-element.4), channel_id=1, replica_groups=mesh['rep'=8,'tp'=4] {'rep'}, use_global_device_ids=true, to_apply=%region_10.11 | all-reduce | flops 1280 | bytes 10240 | tf_op jit(solution)/shard_map/psum | solution.py:81
  121.2 18.0 %reduce-scatter.3.cloned.1.call-done = bf16[160,1280]{1,0:T(8,128)(2,1)} async-done(((bf16[1280,1280]{1,0:T(8,128)(2,1)}), bf16[160,1280]{1,0:T(8,128)(2,1)}) %reduce-scatter.3.cloned.1.call-update) | async-done | bytes 409616 | tf_op jit(solution)/shard_map/reduce_scatter | solution.py:72
  139.2 1.9 convert_element_type.63
  141.1 76.9 %reduce-scatter.5.cloned.1.call-done = bf16[1280,160]{0,1:T(8,128)(2,1)} async-done(((bf16[1280,1280]{0,1:T(8,128)(2,1)}), bf16[1280,160]{0,1:T(8,128)(2,1)}) %reduce-scatter.5.cloned.1.call-update) | async-done | bytes 409616 | tf_op jit(solution)/shard_map/reduce_scatter | solution.py:75
  218.0 1.9 convert_element_type.66
  (4 shorter events, 0.0 us)
Async XLA Ops:
  8.0 22.7 %copy-start = (bf16[1280,1280]{1,0:T(8,128)(2,1)S(1)}, bf16[1280,1280]{1,0:T(8,128)(2,1)}, u32[]{:S(2)}) copy-start(bf16[1280,1280]{1,0:T(8,128)(2,1)} %param.11) | copy-start | bytes 9830404
  8.0 13.0 %copy-start.6 = (s32[4]{0:T(128)S(1)}, s32[4]{0:T(128)}, u32[]{:S(2)}) copy-start(s32[4]{0:T(128)} %param.8) | copy-start | bytes 52
  8.0 13.0 %copy-start.4 = (bf16[4,12,1280]{2,0,1:T(4,128)(2,1)S(1)}, bf16[4,12,1280]{2,0,1:T(4,128)(2,1)}, u32[]{:S(2)}) copy-start(bf16[4,12,1280]{2,0,1:T(4,128)(2,1)} %param.7) | copy-start | bytes 368644
  8.0 13.4 %copy-start.5 = (f32[1280]{0:T(1024)S(1)}, f32[1280]{0:T(1024)}, u32[]{:S(2)}) copy-start(f32[1280]{0:T(1024)} %param.13) | copy-start | bytes 15364
  10.5 14.2 %all-to-all-start = ((s32[8,1,1]{2,1,0:T(1,128)}), s32[8,1,1]{2,1,0:T(1,128)S(1)}, u32[]{:S(2)}, u32[]{:S(2)}) async-start(s32[8,1,1]{2,1,0:T(1,128)} %copy.19), calls=%async_computation | async-start | bytes 8192 | tf_op jit(solution)/shard_map/all_to_all | solution.py:53
  24.7 15.8 %all-to-all-start.1 = ((bf16[8,12,1280]{2,1,0:T(8,128)(2,1)}), bf16[8,12,1280]{2,1,0:T(8,128)(2,1)}, u32[]{:S(2)}, u32[]{:S(2)}) async-start(bf16[8,12,1280]{2,1,0:T(8,128)(2,1)} %copy.20), calls=%async_computation.1 | async-start | bytes 655360 | tf_op jit(solution)/shard_map/all_to_all | solution.py:52
  30.7 62.8 %all-reduce.2.cloned.1.call-start = ((), (), s32[]{:S(2)}) async-start(), calls=%async_computation.4 | async-start | bytes 1966080 | tf_op jit(solution)/shard_map/psum | solution.py:80
  40.5 11.2 %copy-start.7 = (bf16[1280,1280]{1,0:T(8,128)(2,1)S(1)}, bf16[1280,1280]{1,0:T(8,128)(2,1)}, u32[]{:S(2)}) copy-start(bf16[1280,1280]{1,0:T(8,128)(2,1)} %param.12) | copy-start | bytes 9830404
  51.7 3.9 %copy-start.2 = (bf16[8,48,1280]{2,1,0:T(8,128)(2,1)}, bf16[8,48,1280]{2,1,0:T(8,128)(2,1)S(1)}, u32[]{:S(2)}) copy-start(bf16[8,48,1280]{2,1,0:T(8,128)(2,1)S(1)} %copy.22) | copy-start | bytes 2949124
  55.6 1.0 copy-start.8
  59.0 80.2 %reduce-scatter.3.cloned.1.call-start = ((), (), s32[]{:S(2)}) async-start(), calls=%async_computation.5 | async-start | bytes 3686400 | tf_op jit(solution)/shard_map/reduce_scatter | solution.py:72
  64.1 153.9 %reduce-scatter.5.cloned.1.call-start = ((), (), s32[]{:S(2)}) async-start(), calls=%async_computation.6 | async-start | bytes 3686400 | tf_op jit(solution)/shard_map/reduce_scatter | solution.py:75
  93.5 2.6 %copy-start.1 = (bf16[8,48,1280]{2,1,0:T(8,128)(2,1)S(1)}, bf16[8,48,1280]{2,1,0:T(8,128)(2,1)}, u32[]{:S(2)}) copy-start(bf16[8,48,1280]{2,1,0:T(8,128)(2,1)} %param.10) | copy-start | bytes 2949124
  93.5 2.6 %copy-start.3 = (bf16[8,48,1280]{2,1,0:T(8,128)(2,1)S(1)}, bf16[8,48,1280]{2,1,0:T(8,128)(2,1)}, u32[]{:S(2)}) copy-start(bf16[8,48,1280]{2,1,0:T(8,128)(2,1)} %copy-done.2) | copy-start | bytes 2949124
Sparse Core Ops, SparseCore 0:
  59.1 34.3 all-reduce.1
Sparse Core Ops, SparseCore 1:
  64.2 74.9 reduce-scatter.2
  142.6 75.3 reduce-scatter.4
where the time goes:
time: 228 us; the launch traced here: 227 us
  waiting for transfers between devices  124 us (54%)
  blocking collectives  31.8 us (14%)
  matrix products  22.5 us (10%)
  other arithmetic  16.1 us (7%)
  between operations  15.7 us (7%)
  starting transfers between devices  13.6 us (6%)
  local copies, waits for them, and re-layouts  3.62 us (2%)
    reduce_scatter x1, waiting for transfers between devices, local(): lax.psum_scatter(down_local.astype(jnp.bfloat16), 'rep', scatter_dimensio...  76.9 us
    psum x1, waiting for transfers between devices, local(): lax.psum(partial_normed.astype(jnp.bfloat16), 'tp').astype(jnp.float32)  23.6 us
    psum x1, blocking collectives, local(): gain_grads = lax.psum(jnp.sum(grad_normed * centred, axis=0), 'rep')  22.1 us
    reduce_scatter x1, waiting for transfers between devices, local(): lax.psum_scatter(up_local.astype(jnp.bfloat16), 'rep', scatter_dimension=...  18 us
    all_gather x1, blocking collectives, local(): lax.all_gather(compact(inbound, slot_recv, capacity), 'tp', axis=1, tiled...  9.67 us
    all_to_all x1, starting transfers between devices, local(): lax.all_to_all(slot_sent, 'rep', split_axis=0, concat_axis=0, tiled=True)  7.31 us
    all_to_all x1, starting transfers between devices, local(): lax.all_to_all(packed, 'rep', split_axis=0, concat_axis=0, tiled=True)  6 us
    all_to_all x1, waiting for transfers between devices, local(): lax.all_to_all(packed, 'rep', split_axis=0, concat_axis=0, tiled=True)  5.58 us
  transfers between devices with their start and end apart: 5, of which 4 were waited for; matrix products, arithmetic and copies ran while one was open for 13% of the time, Pallas kernels for 0%

commit v1 on v0

--- a/solution.py
+++ b/solution.py
@@ -6,6 +6,22 @@
 epsilon = 1e-05
 gelu_c = 0.7978845608028654
 gelu_a = 0.044715
+
+
+def swapped_with_each(array, axis, split, join):
+    ways, here = (lax.axis_size(axis), lax.axis_index(axis))
+    width = array.shape[split] // ways
+    shape = list(array.shape)
+    shape[split] = width
+    height = shape[join]
+    shape[join] = height * ways
+    full = jnp.zeros(shape, array.dtype)
+    for mask in range(ways):
+        part = lax.dynamic_slice_in_dim(array, (here ^ mask) * width, width, axis=split)
+        if mask:
+            part = lax.ppermute(part, axis, [(d, d ^ mask) for d in range(ways)])
+        full = lax.dynamic_update_slice_in_dim(full, part, (here ^ mask) * height, axis=join)
+    return full
 
 
 def gelu_value(preact):
@@ -50,7 +66,7 @@
     packed, slot_sent = outbound(image_grads, dest_rank, dest_slot, groups, capacity)
     inbound, slot_recv = (
         lax.all_to_all(packed, "rep", split_axis=0, concat_axis=0, tiled=True),
-        lax.all_to_all(slot_sent, "rep", split_axis=0, concat_axis=0, tiled=True),
+        swapped_with_each(slot_sent, "rep", 0, 0),
     )
     routed = lax.all_gather(compact(inbound, slot_recv, capacity), "tp", axis=1, tiled=True)
     rows = capacity * patches

time: 228 us -> 233 us (1.022)
  starting transfers between devices: 13.6 us -> 19.3 us
  local copies, waits for them, and re-layouts: 3.62 us -> 8.78 us
  waiting for transfers between devices: 124 us -> 119 us
    ppermute x0 -> x7, starting transfers between devices: none -> 14.1 us  [swapped_with_each(): part = lax.ppermute(part, axis, [(d, d ^ mask) for d in range(ways)])]
    all_to_all x1 -> x0, starting transfers between devices: 7.31 us -> none  [local(): lax.all_to_all(slot_sent, 'rep', split_axis=0, concat_axis=0, tiled=True)]
    all_to_all x1, waiting for transfers between devices: 5.58 us -> 0.01 us  [local(): lax.all_to_all(packed, 'rep', split_axis=0, concat_axis=0, tiled=True)]
    dynamic_update_slice x0 -> x7, local copies, waits for them, and re-layouts: none -> 5.08 us  [swapped_with_each(): lax.dynamic_update_slice_in_dim(full, part, (here ^ mask) * height, axis=...]
  transfers between devices with their start and end apart: 5 -> 11, of which waited for: 4 -> 4; matrix products, arithmetic and copies ran while one was open for 13% -> 14% of each run, Pallas kernels for 0% -> 0%
where the time goes in v1:
time: 233 us; the launch traced here: 232 us
  waiting for transfers between devices  119 us (51%)
  blocking collectives  31.8 us (14%)
  matrix products  22.2 us (10%)
  starting transfers between devices  19.3 us (8%)
  between operations  15.7 us (7%)
  other arithmetic  14.8 us (6%)
  local copies, waits for them, and re-layouts  8.78 us (4%)
    reduce_scatter x1, waiting for transfers between devices, local(): lax.psum_scatter(down_local.astype(jnp.bfloat16), 'rep', scatter_dimensio...  76.7 us
    psum x1, waiting for transfers between devices, local(): lax.psum(partial_normed.astype(jnp.bfloat16), 'tp').astype(jnp.float32)  23 us
    psum x1, blocking collectives, local(): gain_grads = lax.psum(jnp.sum(grad_normed * centred, axis=0), 'rep')  22.1 us
    reduce_scatter x1, waiting for transfers between devices, local(): lax.psum_scatter(up_local.astype(jnp.bfloat16), 'rep', scatter_dimension=...  18.1 us
    ppermute x7, starting transfers between devices, swapped_with_each(): part = lax.ppermute(part, axis, [(d, d ^ mask) for d in range(ways)])  14.1 us
    all_gather x1, blocking collectives, local(): lax.all_gather(compact(inbound, slot_recv, capacity), 'tp', axis=1, tiled...  9.67 us
    dot_general x1, matrix products, local(): down_local = jnp.dot(hidden.T, grads, preferred_element_type=jnp.float32)  5.52 us
    dot_general x1, matrix products, local(): up_local = jnp.dot(normed.T, grad_pre, preferred_element_type=jnp.float32)  5.09 us
  transfers between devices with their start and end apart: 11, of which 4 were waited for; matrix products, arithmetic and copies ran while one was open for 14% of the time, Pallas kernels for 0%

profile of v1, /device:TPU:0, one launch (start us, length us, event | category | flops | bytes accessed | tf_op | source)
XLA Modules:
  0.0 231.8 jit_solution(4553498923756590631)
XLA Ops:
  8.0 0.0 copy-start
  8.1 0.9 fusion.26
  8.9 0.8 select_reduce_fusion
  9.8 0.8 fusion.33
  10.6 3.0 %collective-permute-start = (s32[1]{0:T(128)}, s32[1]{0:T(128)}, u32[]{:S(2)}, u32[]{:S(2)}) collective-permute-start(s32[1]{0:T(128)} %get-tuple-element.13), channel_id=1, source_target_pairs={{0,4},{4,0},{8,12},{12,8},{16,20},{20,16},{24,28},{28,24},{1,5},{5... | collective-permute-start | bytes 20 | tf_op jit(solution)/shard_map/ppermute | solution.py:22
  13.6 1.6 collective-permute-start.1
  15.1 0.0 collective-permute-start.2
  15.1 3.0 %collective-permute-start.3 = (s32[1]{0:T(128)}, s32[1]{0:T(128)}, u32[]{:S(2)}, u32[]{:S(2)}) collective-permute-start(s32[1]{0:T(128)} %get-tuple-element.10), channel_id=1, source_target_pairs={{0,16},{4,20},{8,24},{12,28},{16,0},{20,4},{24,8},{28,12},{1,17},{... | collective-permute-start | bytes 20 | tf_op jit(solution)/shard_map/ppermute | solution.py:22
  18.1 1.3 collective-permute-start.4
  19.4 1.2 convolution_convert_fusion.4
  20.7 0.8 copy.14
  21.4 4.9 %all-to-all-start = ((bf16[8,12,1280]{2,1,0:T(8,128)(2,1)}), bf16[8,12,1280]{2,1,0:T(8,128)(2,1)}, u32[]{:S(2)}, u32[]{:S(2)}) async-start(bf16[8,12,1280]{2,1,0:T(8,128)(2,1)} %copy.14), calls=%async_computation | async-start | bytes 655360 | tf_op jit(solution)/shard_map/all_to_all | solution.py:68
  26.3 0.0 all-reduce.2.cloned.1.call-start
  26.3 1.4 convert_reduce_fusion
  27.8 1.6 multiply_reduce_fusion
  29.4 0.1 div.18
  29.5 0.1 sqrt.6
  29.5 0.0 copy-done.5
  29.5 1.6 multiply_convert_fusion.1
  31.1 0.0 copy-done
  31.1 0.0 copy-start.4
  31.1 2.8 %fusion.34 = f32[384,1280]{1,0:T(8,128)} fusion(bf16[384,1280]{1,0:T(8,128)(2,1)S(1)} %multiply_convert_fusion.1, bf16[1280,1280]{1,0:T(8,128)(2,1)S(1)} %copy-done), kind=kOutput, calls=%fused_computation.58 | convolution fusion | flops 1258291200 | bytes 6225920 | tf_op jit(solution)/shard_map/dot_general | solution.py:80
  33.9 0.0 collective-permute-done
  33.9 3.8 %collective-permute-start.5 = (s32[1]{0:T(128)}, s32[1]{0:T(128)}, u32[]{:S(2)}, u32[]{:S(2)}) collective-permute-start(s32[1]{0:T(128)} %get-tuple-element.8), channel_id=1, source_target_pairs={{0,24},{4,28},{8,16},{12,20},{16,8},{20,12},{24,0},{28,4},{1,25},{... | collective-permute-start | bytes 20 | tf_op jit(solution)/shard_map/ppermute | solution.py:22
  37.7 0.7 dynamic_update_slice.41
  38.4 0.0 collective-permute-done.1
  38.4 1.5 collective-permute-start.6
  39.8 0.7 dynamic_update_slice.42
  40.5 0.0 collective-permute-done.2
  40.5 0.7 dynamic_update_slice.43
  41.3 0.0 collective-permute-done.3
  41.3 0.7 dynamic_update_slice.44
  42.0 0.0 collective-permute-done.4
  42.0 0.7 dynamic_update_slice.45
  42.8 0.0 collective-permute-done.5
  42.8 0.8 dynamic_update_slice.46
  43.5 1.3 collective-permute-done.6
  44.9 0.7 dynamic_update_slice.47
  45.6 0.0 all-to-all-done
  45.6 1.3 convolution_convert_fusion.3
  47.0 9.7 %all_gather.3 = bf16[8,48,1280]{2,0,1:T(8,128)(2,1)S(1)} all-gather(bf16[8,12,1280]{2,0,1:T(8,128)(2,1)S(1)} %convolution_convert_fusion.3), channel_id=1, replica_groups=mesh['rep'=8,'tp'=4] {'tp'}, dimensions={1}, use_global_device_ids=true | all-gather | bytes 1228800 | tf_op jit(solution)/shard_map/all_gather | solution.py:71
  56.6 0.2 copy.16
  56.8 3.8 %fusion = bf16[384,1280]{1,0:T(8,128)(2,1)S(1)} fusion(bf16[384,1280]{1,0:T(8,128)(2,1)S(1)} %bitcast.31, bf16[1280,1280]{1,0:T(8,128)(2,1)S(1)} %copy-done.6, f32[384,1280]{1,0:T(8,128)} %fusion.34), kind=kOutput, calls=%fused_computation.5 | convolution fusion | flops 1267630080 | bytes 7208960 | tf_op jit(solution)/shard_map/dot_general | solution.py:82
  60.7 0.0 copy-done.2
  60.7 0.0 copy-start.7
  60.7 0.9 copy-done.7
  61.6 2.4 %convolution_convert_fusion.2 = bf16[384,1280]{1,0:T(8,128)(2,1)} fusion(bf16[384,1280]{1,0:T(8,128)(2,1)S(1)} %fusion, bf16[1280,1280]{1,0:T(8,128)(2,1)S(1)} %copy-done), kind=kOutput, calls=%fused_computation.6 | convolution fusion | flops 1258782720 | bytes 5242880 | tf_op jit(solution)/shard_map/dot_general | solution.py:86
  64.0 0.0 all-reduce.2.cloned.1.call-update
  64.1 0.0 reduce-scatter.3.cloned.1.call-start
  64.1 5.1 %convolution_convert_fusion.1 = bf16[1280,1280]{1,0:T(8,128)(2,1)} fusion(bf16[384,1280]{1,0:T(8,128)(2,1)} %copy-done.4, bf16[384,1280]{1,0:T(8,128)(2,1)} %copy-done.7), kind=kOutput, calls=%fused_computation.1 | convolution fusion | flops 1259929600 | bytes 5242880 | tf_op jit(solution)/shard_map/dot_general | solution.py:85
  69.2 0.0 reduce-scatter.3.cloned.1.call-update
  69.2 0.2 reduce-scatter.5.cloned.1.call-start
  69.5 5.5 %convolution_convert_fusion = bf16[1280,1280]{0,1:T(8,128)(2,1)} fusion(bf16[384,1280]{1,0:T(8,128)(2,1)} %bitcast.32, f32[384,1280]{1,0:T(8,128)} %fusion.34), kind=kOutput, calls=%fused_computation | convolution fusion | flops 1264353280 | bytes 6225920 | tf_op jit(solution)/shard_map/dot_general | solution.py:84
  75.0 0.0 reduce-scatter.5.cloned.1.call-update
  75.0 23.0 %all-reduce.2.cloned.1.call-done = bf16[384,1280]{1,0:T(8,128)(2,1)} async-done(((bf16[384,1280]{1,0:T(8,128)(2,1)}), bf16[384,1280]{1,0:T(8,128)(2,1)}) %all-reduce.2.cloned.1.call-update) | async-done | bytes 983056 | tf_op jit(solution)/shard_map/psum | solution.py:96
  98.1 2.6 %fusion.8 = (f32[1280]{0:T(1024)S(1)}, f32[384]{0:T(512)S(1)}, f32[384]{0:T(512)S(1)}) fusion(bf16[384,1280]{1,0:T(8,128)(2,1)} %all-reduce.2.cloned.1.call-done, bf16[8,48,1280]{2,1,0:T(8,128)(2,1)} %param.10, f32[384]{0:T(512)S(1)} %div.18, f32[384]{0:T(512)S(1)} %sqrt.6, f32[1280]{0:T(1024)S(1)} %copy-done.5), kind=kLoop, calls=%fused_computation.18 | loop fusion | flops 4913152 | bytes 1982464 | tf_op jit(solution)/shard_map/reduce_sum | solution.py:97
  100.7 2.1 fusion.6
  102.7 0.1 constant_dynamic-slice_fusion
  102.8 0.8 copy.22
  103.6 22.1 %psum.15 = f32[1280]{0:T(1024)} all-reduce(f32[1280]{0:T(1024)S(1)} %get-tuple-element.4), channel_id=1, replica_groups=mesh['rep'=8,'tp'=4] {'rep'}, use_global_device_ids=true, to_apply=%region_10.11 | all-reduce | flops 1280 | bytes 10240 | tf_op jit(solution)/shard_map/psum | solution.py:97
  125.7 18.1 %reduce-scatter.3.cloned.1.call-done = bf16[160,1280]{1,0:T(8,128)(2,1)} async-done(((bf16[1280,1280]{1,0:T(8,128)(2,1)}), bf16[160,1280]{1,0:T(8,128)(2,1)}) %reduce-scatter.3.cloned.1.call-update) | async-done | bytes 409616 | tf_op jit(solution)/shard_map/reduce_scatter | solution.py:88
  143.8 1.9 convert_element_type.63
  145.8 76.7 %reduce-scatter.5.cloned.1.call-done = bf16[1280,160]{0,1:T(8,128)(2,1)} async-done(((bf16[1280,1280]{0,1:T(8,128)(2,1)}), bf16[1280,160]{0,1:T(8,128)(2,1)}) %reduce-scatter.5.cloned.1.call-update) | async-done | bytes 409616 | tf_op jit(solution)/shard_map/reduce_scatter | solution.py:91
  222.4 1.9 convert_element_type.66
  (14 shorter events, 0.0 us)
Async XLA Ops:
  8.0 23.1 %copy-start = (bf16[1280,1280]{1,0:T(8,128)(2,1)S(1)}, bf16[1280,1280]{1,0:T(8,128)(2,1)}, u32[]{:S(2)}) copy-start(bf16[1280,1280]{1,0:T(8,128)(2,1)} %param.11) | copy-start | bytes 9830404
  8.0 21.5 %copy-start.5 = (f32[1280]{0:T(1024)S(1)}, f32[1280]{0:T(1024)}, u32[]{:S(2)}) copy-start(f32[1280]{0:T(1024)} %param.13) | copy-start | bytes 15364
  10.6 23.4 %collective-permute-start = (s32[1]{0:T(128)}, s32[1]{0:T(128)}, u32[]{:S(2)}, u32[]{:S(2)}) collective-permute-start(s32[1]{0:T(128)} %get-tuple-element.13), channel_id=1, source_target_pairs={{0,4},{4,0},{8,12},{12,8},{16,20},{20,16},{24,28},{28,24},{1,5},{5... | collective-permute-start | bytes 20 | tf_op jit(solution)/shard_map/ppermute | solution.py:22
  13.6 24.8 %collective-permute-start.1 = (s32[1]{0:T(128)}, s32[1]{0:T(128)}, u32[]{:S(2)}, u32[]{:S(2)}) collective-permute-start(s32[1]{0:T(128)} %get-tuple-element.12), channel_id=1, source_target_pairs={{0,8},{4,12},{8,0},{12,4},{16,24},{20,28},{24,16},{28,20},{1,9},{5... | collective-permute-start | bytes 20 | tf_op jit(solution)/shard_map/ppermute | solution.py:22
  15.1 25.4 %collective-permute-start.2 = (s32[1]{0:T(128)}, s32[1]{0:T(128)}, u32[]{:S(2)}, u32[]{:S(2)}) collective-permute-start(s32[1]{0:T(128)} %get-tuple-element.11), channel_id=1, source_target_pairs={{0,12},{4,8},{8,4},{12,0},{16,28},{20,24},{24,20},{28,16},{1,13},{... | collective-permute-start | bytes 20 | tf_op jit(solution)/shard_map/ppermute | solution.py:22
  15.1 26.1 %collective-permute-start.3 = (s32[1]{0:T(128)}, s32[1]{0:T(128)}, u32[]{:S(2)}, u32[]{:S(2)}) collective-permute-start(s32[1]{0:T(128)} %get-tuple-element.10), channel_id=1, source_target_pairs={{0,16},{4,20},{8,24},{12,28},{16,0},{20,4},{24,8},{28,12},{1,17},{... | collective-permute-start | bytes 20 | tf_op jit(solution)/shard_map/ppermute | solution.py:22
  18.1 23.9 %collective-permute-start.4 = (s32[1]{0:T(128)}, s32[1]{0:T(128)}, u32[]{:S(2)}, u32[]{:S(2)}) collective-permute-start(s32[1]{0:T(128)} %get-tuple-element.9), channel_id=1, source_target_pairs={{0,20},{4,16},{8,28},{12,24},{16,4},{20,0},{24,12},{28,8},{1,21},{... | collective-permute-start | bytes 20 | tf_op jit(solution)/shard_map/ppermute | solution.py:22
  21.4 24.2 %all-to-all-start = ((bf16[8,12,1280]{2,1,0:T(8,128)(2,1)}), bf16[8,12,1280]{2,1,0:T(8,128)(2,1)}, u32[]{:S(2)}, u32[]{:S(2)}) async-start(bf16[8,12,1280]{2,1,0:T(8,128)(2,1)} %copy.14), calls=%async_computation | async-start | bytes 655360 | tf_op jit(solution)/shard_map/all_to_all | solution.py:68
  26.3 71.8 %all-reduce.2.cloned.1.call-start = ((), (), s32[]{:S(2)}) async-start(), calls=%async_computation.3 | async-start | bytes 1966080 | tf_op jit(solution)/shard_map/psum | solution.py:96
  31.1 2.8 %copy-start.4 = (bf16[384,1280]{1,0:T(8,128)(2,1)}, bf16[384,1280]{1,0:T(8,128)(2,1)S(1)}, u32[]{:S(2)}) copy-start(bf16[384,1280]{1,0:T(8,128)(2,1)S(1)} %multiply_convert_fusion.1) | copy-start | bytes 2949124
  33.9 8.8 %collective-permute-start.5 = (s32[1]{0:T(128)}, s32[1]{0:T(128)}, u32[]{:S(2)}, u32[]{:S(2)}) collective-permute-start(s32[1]{0:T(128)} %get-tuple-element.8), channel_id=1, source_target_pairs={{0,24},{4,28},{8,16},{12,20},{16,8},{20,12},{24,0},{28,4},{1,25},{... | collective-permute-start | bytes 20 | tf_op jit(solution)/shard_map/ppermute | solution.py:22
  38.4 6.5 %collective-permute-start.6 = (s32[1]{0:T(128)}, s32[1]{0:T(128)}, u32[]{:S(2)}, u32[]{:S(2)}) collective-permute-start(s32[1]{0:T(128)} %get-tuple-element.7), channel_id=1, source_target_pairs={{0,28},{4,24},{8,20},{12,16},{16,12},{20,8},{24,4},{28,0},{1,29},{... | collective-permute-start | bytes 20 | tf_op jit(solution)/shard_map/ppermute | solution.py:22
  45.6 11.2 %copy-start.6 = (bf16[1280,1280]{1,0:T(8,128)(2,1)S(1)}, bf16[1280,1280]{1,0:T(8,128)(2,1)}, u32[]{:S(2)}) copy-start(bf16[1280,1280]{1,0:T(8,128)(2,1)} %param.12) | copy-start | bytes 9830404
  56.8 3.9 %copy-start.2 = (bf16[8,48,1280]{2,1,0:T(8,128)(2,1)}, bf16[8,48,1280]{2,1,0:T(8,128)(2,1)S(1)}, u32[]{:S(2)}) copy-start(bf16[8,48,1280]{2,1,0:T(8,128)(2,1)S(1)} %copy.16) | copy-start | bytes 2949124
  60.7 1.0 copy-start.7
  64.1 79.7 %reduce-scatter.3.cloned.1.call-start = ((), (), s32[]{:S(2)}) async-start(), calls=%async_computation.4 | async-start | bytes 3686400 | tf_op jit(solution)/shard_map/reduce_scatter | solution.py:88
  69.2 153.2 %reduce-scatter.5.cloned.1.call-start = ((), (), s32[]{:S(2)}) async-start(), calls=%async_computation.5 | async-start | bytes 3686400 | tf_op jit(solution)/shard_map/reduce_scatter | solution.py:91
  98.1 2.6 %copy-start.1 = (bf16[8,48,1280]{2,1,0:T(8,128)(2,1)S(1)}, bf16[8,48,1280]{2,1,0:T(8,128)(2,1)}, u32[]{:S(2)}) copy-start(bf16[8,48,1280]{2,1,0:T(8,128)(2,1)} %param.10) | copy-start | bytes 2949124
  98.1 2.6 %copy-start.3 = (bf16[8,48,1280]{2,1,0:T(8,128)(2,1)S(1)}, bf16[8,48,1280]{2,1,0:T(8,128)(2,1)}, u32[]{:S(2)}) copy-start(bf16[8,48,1280]{2,1,0:T(8,128)(2,1)} %copy-done.2) | copy-start | bytes 2949124
Sparse Core Ops, SparseCore 0:
  64.2 33.8 all-reduce.1
Sparse Core Ops, SparseCore 1:
  69.3 74.4 reduce-scatter.2
  147.3 75.1 reduce-scatter.4
